TPU v7x, 32 devices: a whole 2x2x4 slice. The times are simulated.
32 devices in a mesh: dp: 2 (over x), node: 4 (over z), local: 4 (over y, core).
Axes of the slice: x: 2, y: 2, z: 4, core: 2. Of those that a mesh axis runs over, the one named last changes fastest.
Arguments:
- tokens: bfloat16 [6144, 2048], P(('dp', 'node', 'local')), may hold values from -6 to 6
- cotangent: bfloat16 [6144, 2048], P(('dp', 'node', 'local')), may hold values from -6 to 6
- expert_of: int32 [6144, 1], P(('dp', 'node', 'local')), may hold values from 0 to 3; in each aligned block of 192 rows (0 to 191, 192 to 383, ...) at most 60 rows name the same one
- w1_codes: bfloat16 [4, 2048, 512], P('local', 'node'), may hold values from -4 to 4
- w1_scales: bfloat16 [4, 64, 512], P('local', 'node'), may hold values from 0.010986328 to 0.044921875
Outputs:
- grad_w2: bfloat16 [4, 2048, 512], P('local', 'node')
Inputs may be any that keep to these rules, and one draw needn't show every extreme that they name: `expert_of`: within the rows of one device (aligned blocks of 192 rows) no expert is named by more than 60 rows, a bound that some block reaches.
All inputs are finite; a program needn't handle non-finite values.
Results may differ from a plain program's by a relative error of at most 0.018.
Values may be sent and summed in bfloat16 or wider, within the bound.
No kernel may reach another device: no remote copies, remote signals or barrier semaphores. Data moves between devices by JAX's collectives and lax.ppermute only.
A program may use at most 64 MiB of HBM per device.

v0:
```python
import jax
import jax.numpy as jnp
from jax import lax
from jax.sharding import PartitionSpec as P

QB = 32


def slot_of(expert_ids, experts, capacity):
    chosen = expert_ids[:, 0]
    onehot = (chosen[:, None] == jnp.arange(experts, dtype=jnp.int32)[None, :]).astype(jnp.int32)
    ranking = jnp.sum((jnp.cumsum(onehot, axis=0) - 1) * onehot, axis=1)
    return chosen * capacity + ranking


def place(row_data, slots, experts, capacity):
    blank_rows = jnp.zeros((experts * capacity, row_data.shape[1]), row_data.dtype)
    return blank_rows.at[slots].set(row_data).reshape(experts, capacity, row_data.shape[1])


def dequant_piece(piece_codes, piece_scales):
    product = piece_codes.astype(jnp.float32) * piece_scales[:, None, :].astype(jnp.float32)
    return product.astype(jnp.bfloat16).reshape(piece_codes.shape[0] * QB, piece_codes.shape[2])


def contract_rows(left_rows, right_rows):
    return lax.dot_general(
        left_rows, right_rows, (((0,), (0,)), ((), ())), preferred_element_type=jnp.float32
    )


def on_device(tokens, cotangent, expert_of, w1_codes, w1_scales):
    experts = lax.axis_size("local")
    tok_dev = tokens.shape[0]
    features = tokens.shape[1]
    capacity = 5 * tok_dev // (4 * experts)
    slots = slot_of(expert_of, experts, capacity)
    sent_x = place(tokens, slots, experts, capacity)
    sent_dy = place(cotangent, slots, experts, capacity)
    got_x, got_dy = (
        lax.all_to_all(sent_x, "local", split_axis=0, concat_axis=0, tiled=True),
        lax.all_to_all(sent_dy, "local", split_axis=0, concat_axis=0, tiled=True),
    )
    served = experts * capacity
    rows_x = got_x.reshape(served, features)
    rows_dy = got_dy.reshape(served, features)
    hidden = w1_codes.shape[2]
    shard_rows = w1_codes.shape[1]
    blocks = shard_rows // QB
    code_up = w1_codes.reshape(blocks, QB, hidden)
    scale_up = w1_scales.reshape(blocks, hidden)
    up_piece = dequant_piece(
        lax.all_gather(code_up, "node", axis=0, tiled=True),
        lax.all_gather(scale_up, "node", axis=0, tiled=True),
    )
    pre = jnp.dot(rows_x, up_piece, preferred_element_type=jnp.float32)
    act = jax.nn.silu(pre).astype(jnp.bfloat16)
    factor = float(tok_dev * lax.axis_size("dp") * lax.axis_size("node")) ** (-0.5)
    second = contract_rows(rows_dy, act)
    rounded = (second * factor).astype(jnp.bfloat16)
    rounded = lax.optimization_barrier(rounded)
    grad_terms = rounded.astype(jnp.float32)
    partial_rows = lax.psum_scatter(
        grad_terms.astype(jnp.bfloat16), "node", scatter_dimension=0, tiled=True
    )
    result = lax.psum(partial_rows, "dp")
    return result[None]


def solution(mesh):
    in_specs = (
        P(("dp", "node", "local"), None),
        P(("dp", "node", "local"), None),
        P(("dp", "node", "local"), None),
        P("local", "node", None),
        P("local", "node", None),
    )
    out_specs = P("local", "node", None)
    return jax.shard_map(
        on_device, mesh=mesh, in_specs=in_specs, out_specs=out_specs, check_vma=False
    )
```

profile of v0, /device:TPU:0, one launch (start us, length us, event | category | flops | bytes accessed | tf_op | source)
XLA Modules:
  0.0 145.8 jit_solution(5696499167571732172)
XLA Ops:
  6.5 0.0 all-gather.3.cloned.1.call-start
  6.5 0.7 all-gather.3.cloned.1.call-update
  7.3 0.7 iota_compare_fusion
  8.0 1.2 reduce-window.6
  9.2 0.1 slice.12
  9.3 0.1 copy.10
  9.4 0.1 copy.11
  9.5 0.1 add_bitcast_fusion
  9.6 0.7 fusion.6
  10.3 0.7 compare_select_fusion
  11.0 2.6 %scatter_custom_fusion.1 = bf16[240,2048]{1,0:T(8,128)(2,1)S(1)} fusion(s32[192]{0:T(256)S(1)} %bitcast.31, bf16[192,2048]{1,0:T(8,128)(2,1)} %param.5, bf16[]{:T(256)} %constant.6.clone.1), kind=kCustom, calls=%fused_computation.5 | custom fusion | bytes 983552 | tf_op jit(solution)/shard_map/scatter | solution.py:18
  13.6 1.2 reshape.39
  14.8 4.3 %all-to-all-start.1 = ((bf16[4,60,2048]{2,1,0:T(8,128)(2,1)}), bf16[4,60,2048]{2,1,0:T(8,128)(2,1)S(1)}, u32[]{:S(2)}, u32[]{:S(2)}) async-start(bf16[4,60,2048]{2,1,0:T(8,128)(2,1)} %reshape.39), calls=%async_computation.1 | async-start | bytes 2097152 | tf_op jit(solution)/shard_map/all_to_all | solution.py:41
  19.0 2.6 %scatter_custom_fusion = bf16[240,2048]{1,0:T(8,128)(2,1)S(1)} fusion(s32[192]{0:T(256)S(1)} %bitcast.32, bf16[192,2048]{1,0:T(8,128)(2,1)} %param.6, bf16[]{:T(256)} %constant.6.clone.1), kind=kCustom, calls=%fused_computation.7 | custom fusion | bytes 983552 | tf_op jit(solution)/shard_map/scatter | solution.py:18
  21.7 0.0 copy-start
  21.7 1.2 reshape.37
  22.9 10.6 %all-to-all-done.1 = bf16[4,60,2048]{2,1,0:T(8,128)(2,1)S(1)} async-done(((bf16[4,60,2048]{2,1,0:T(8,128)(2,1)}), bf16[4,60,2048]{2,1,0:T(8,128)(2,1)S(1)}, u32[]{:S(2)}, u32[]{:S(2)}) %all-to-all-start.1) | async-done | bytes 983072 | tf_op jit(solution)/shard_map/all_to_all | solution.py:41
  33.5 3.5 %all-to-all-start = ((bf16[4,60,2048]{2,1,0:T(8,128)(2,1)}), bf16[4,60,2048]{2,1,0:T(8,128)(2,1)S(1)}, u32[]{:S(2)}, u32[]{:S(2)}) async-start(bf16[4,60,2048]{2,1,0:T(8,128)(2,1)} %reshape.37), calls=%async_computation | async-start | bytes 2097152 | tf_op jit(solution)/shard_map/all_to_all | solution.py:42
  37.0 0.0 reduce-scatter.2.cloned.1.call-start
  37.1 14.8 %all-gather = bf16[1,64,512]{2,1,0:T(8,128)(2,1)S(1)} all-gather(bf16[1,16,512]{2,1,0:T(8,128)(2,1)S(1)} %copy-done), channel_id=2, replica_groups=mesh['dp'=2,'node'=4,'local'=4] {'node'}, dimensions={1}, use_global_device_ids=true | all-gather | bytes 81920 | tf_op jit(solution)/shard_map/all_gather | solution.py:54
  51.8 0.2 reshape.40
  52.0 0.0 all-to-all-done
  52.0 1.2 reshape.38
  53.2 5.2 %all-gather.3.cloned.1.call-done = bf16[64,32,512]{2,1,0:T(8,128)(2,1)} async-done(((bf16[16,32,512]{2,1,0:T(8,128)(2,1)}), bf16[64,32,512]{2,1,0:T(8,128)(2,1)}) %all-gather.3.cloned.1.call-update) | async-done | bytes 2097168 | tf_op jit(solution)/shard_map/all_gather | solution.py:53
  58.4 2.2 %multiply_convert_fusion.1 = bf16[64,32,512]{2,1,0:T(8,128)(2,1)S(1)} fusion(bf16[64,32,512]{2,1,0:T(8,128)(2,1)} %all-gather.3.cloned.1.call-done, f32[64,512]{1,0:T(8,128)S(1)} %bitcast_convert_fusion), kind=kLoop, calls=%fused_computation.3 | loop fusion | flops 3145728 | bytes 4325376 | tf_op jit(solution)/shard_map/convert_element_type | solution.py:23
  60.6 4.0 %multiply_convert_fusion = bf16[2048,512]{1,0:T(8,128)(2,1)} fusion(bf16[240,2048]{1,0:T(8,128)(2,1)} %reshape.38, bf16[240,2048]{1,0:T(8,128)(2,1)S(1)} %reshape.40, bf16[2048,512]{1,0:T(8,128)(2,1)S(1)} %bitcast.23), kind=kOutput, calls=%fused_computation.2 | convolution fusion | flops 1009344512 | bytes 6160384 | tf_op jit(solution)/shard_map/dot_general | solution.py:27
  64.6 0.0 reduce-scatter.2.cloned.1.call-update
  64.6 0.0 all-reduce.3.cloned.1.call-start
  64.7 42.5 %reduce-scatter.2.cloned.1.call-done = bf16[512,512]{1,0:T(8,128)(2,1)} async-done(((bf16[2048,512]{1,0:T(8,128)(2,1)}), bf16[512,512]{1,0:T(8,128)(2,1)}) %reduce-scatter.2.cloned.1.call-update) | async-done | bytes 524304 | tf_op jit(solution)/shard_map/reduce_scatter | solution.py:63
  107.2 0.0 all-reduce.3.cloned.1.call-update
  107.2 30.2 %all-reduce.3.cloned.1.call-done = bf16[1,512,512]{2,1,0:T(8,128)(2,1)} async-done(((bf16[1,512,512]{2,1,0:T(8,128)(2,1)}), bf16[1,512,512]{2,1,0:T(8,128)(2,1)}) %all-reduce.3.cloned.1.call-update) | async-done | bytes 524304 | tf_op jit(solution)/shard_map/psum | solution.py:66
  137.4 1.9 %copy.16 = bf16[1,512,512]{2,1,0:T(8,128)(2,1)} copy(bf16[1,512,512]{2,1,0:T(8,128)(2,1)} %all-reduce.3.cloned.1.call-done) | data formatting | bytes 1048576
  (7 shorter events, 0.1 us)
Async XLA Ops:
  6.5 51.8 %all-gather.3.cloned.1.call-start = ((), (), s32[]{:S(2)}) async-start(), calls=%async_computation.3 | async-start | bytes 2621440 | tf_op jit(solution)/shard_map/all_gather | solution.py:53
  14.8 18.7 %all-to-all-start.1 = ((bf16[4,60,2048]{2,1,0:T(8,128)(2,1)}), bf16[4,60,2048]{2,1,0:T(8,128)(2,1)S(1)}, u32[]{:S(2)}, u32[]{:S(2)}) async-start(bf16[4,60,2048]{2,1,0:T(8,128)(2,1)} %reshape.39), calls=%async_computation.1 | async-start | bytes 2097152 | tf_op jit(solution)/shard_map/all_to_all | solution.py:41
  21.7 15.4 %copy-start = (bf16[1,16,512]{2,1,0:T(8,128)(2,1)S(1)}, bf16[1,16,512]{2,1,0:T(8,128)(2,1)}, u32[]{:S(2)}) copy-start(bf16[1,16,512]{2,1,0:T(8,128)(2,1)} %param.9) | copy-start | bytes 49156
  33.5 18.6 %all-to-all-start = ((bf16[4,60,2048]{2,1,0:T(8,128)(2,1)}), bf16[4,60,2048]{2,1,0:T(8,128)(2,1)S(1)}, u32[]{:S(2)}, u32[]{:S(2)}) async-start(bf16[4,60,2048]{2,1,0:T(8,128)(2,1)} %reshape.37), calls=%async_computation | async-start | bytes 2097152 | tf_op jit(solution)/shard_map/all_to_all | solution.py:42
  37.0 70.2 %reduce-scatter.2.cloned.1.call-start = ((), (), s32[]{:S(2)}) async-start(), calls=%async_computation.4 | async-start | bytes 2621440 | tf_op jit(solution)/shard_map/reduce_scatter | solution.py:63
  64.6 72.8 %all-reduce.3.cloned.1.call-start = ((), (), s32[]{:S(2)}) async-start(), calls=%async_computation.5 | async-start | bytes 1048576 | tf_op jit(solution)/shard_map/psum | solution.py:66
Sparse Core Ops, SparseCore 0:
  8.9 49.4 all-gather.2
  64.7 42.4 reduce-scatter.1
  109.5 27.8 all-reduce.2
where the time goes:
time: 146 us
  waiting for transfers between devices  89.2 us (61%)
  blocking collectives  14.8 us (10%)
  between operations  13.2 us (9%)
  local copies, waits for them, and re-layouts  11.1 us (8%)
  starting transfers between devices  7.87 us (5%)
  other arithmetic  5.63 us (4%)
  matrix products  4 us (3%)
    reduce_scatter x1, waiting for transfers between devices, on_device(): lax.psum_scatter(grad_terms.astype(jnp.bfloat16), 'node', scatter_dimensi...  42.5 us
    psum x1, waiting for transfers between devices, on_device(): result = lax.psum(partial_rows, 'dp')  30.2 us
    all_gather x1, blocking collectives, on_device(): lax.all_gather(scale_up, 'node', axis=0, tiled=True)  14.8 us
    all_to_all x1, waiting for transfers between devices, on_device(): lax.all_to_all(sent_x, 'local', split_axis=0, concat_axis=0, tiled=True)  10.6 us
    scatter x2, local copies, waits for them, and re-layouts, place(): blank_rows.at[slots].set(row_data)  5.25 us
    all_gather x1, waiting for transfers between devices, on_device(): lax.all_gather(code_up, 'node', axis=0, tiled=True)  5.17 us
    all_to_all x1, starting transfers between devices, on_device(): lax.all_to_all(sent_x, 'local', split_axis=0, concat_axis=0, tiled=True)  4.26 us
    dot_general x1, matrix products, contract_rows(): lax.dot_general(left_rows, right_rows, (((0,), (0,)), ((), ())), preferre...  4 us
  transfers between devices with their start and end apart: 5, of which 4 were waited for; matrix products, arithmetic and copies ran while one was open for 9% of the time, Pallas kernels for 0%

commit v1 on v0

--- a/solution.py
+++ b/solution.py
@@ -63,7 +63,8 @@
     partial_rows = lax.psum_scatter(
         grad_terms.astype(jnp.bfloat16), "node", scatter_dimension=0, tiled=True
     )
-    result = lax.psum(partial_rows, "dp")
+    produce_the_routes_all = lambda s0: jnp.sum(lax.all_gather(s0, axis_name="dp"), axis=0)
+    result = produce_the_routes_all(partial_rows)
     return result[None]
 
 

time: 146 us -> 139 us (0.952)
  waiting for transfers between devices: 89.2 us -> 81.1 us
  other arithmetic: 5.63 us -> 7.97 us
  local copies, waits for them, and re-layouts: 11.1 us -> 9.24 us
    psum x1 -> x0, waiting for transfers between devices: 30.2 us -> none  [on_device(): result = lax.psum(partial_rows, 'dp')]
    all_gather x0 -> x1, waiting for transfers between devices: none -> 22 us  [on_device(): lax.all_gather(s0, axis_name='dp')]
    reduce_sum x0 -> x1, other arithmetic: none -> 2.35 us  [on_device(): jnp.sum(lax.all_gather(s0, axis_name='dp'), axis=0)]
    unnamed x4 -> x3, local copies, waits for them, and re-layouts: 1.88 us -> 0.01 us
where the time goes in v1:
time: 139 us; the launch traced here: 138 us
  waiting for transfers between devices  81.1 us (58%)
  blocking collectives  14.8 us (11%)
  between operations  13.2 us (9%)
  local copies, waits for them, and re-layouts  9.24 us (7%)
  other arithmetic  7.97 us (6%)
  starting transfers between devices  7.87 us (6%)
  matrix products  4 us (3%)
    reduce_scatter x1, waiting for transfers between devices, on_device(): lax.psum_scatter(grad_terms.astype(jnp.bfloat16), 'node', scatter_dimensi...  42.5 us
    all_gather x1, waiting for transfers between devices, on_device(): lax.all_gather(s0, axis_name='dp')  22 us
    all_gather x1, blocking collectives, on_device(): lax.all_gather(scale_up, 'node', axis=0, tiled=True)  14.8 us
    all_to_all x1, waiting for transfers between devices, on_device(): lax.all_to_all(sent_x, 'local', split_axis=0, concat_axis=0, tiled=True)  10.6 us
    scatter x2, local copies, waits for them, and re-layouts, place(): blank_rows.at[slots].set(row_data)  5.25 us
    all_gather x1, waiting for transfers between devices, on_device(): lax.all_gather(code_up, 'node', axis=0, tiled=True)  5.17 us
    all_to_all x1, starting transfers between devices, on_device(): lax.all_to_all(sent_x, 'local', split_axis=0, concat_axis=0, tiled=True)  4.26 us
    dot_general x1, matrix products, contract_rows(): lax.dot_general(left_rows, right_rows, (((0,), (0,)), ((), ())), preferre...  4 us
  transfers between devices with their start and end apart: 5, of which 4 were waited for; matrix products, arithmetic and copies ran while one was open for 9% of the time, Pallas kernels for 0%

profile of v1, /device:TPU:0, one launch (start us, length us, event | category | flops | bytes accessed | tf_op | source)
XLA Modules:
  0.0 138.1 jit_solution(1387920841038282267)
XLA Ops:
  6.5 0.0 all-gather.5.cloned.1.call-start
  6.5 0.7 all-gather.5.cloned.1.call-update
  7.3 0.7 iota_compare_fusion
  8.0 1.2 reduce-window.6
  9.2 0.1 slice.12
  9.3 0.1 copy.10
  9.4 0.1 copy.11
  9.5 0.1 add_bitcast_fusion
  9.6 0.7 fusion.6
  10.3 0.7 compare_select_fusion
  11.0 2.6 %scatter_custom_fusion.1 = bf16[240,2048]{1,0:T(8,128)(2,1)S(1)} fusion(s32[192]{0:T(256)S(1)} %bitcast.32, bf16[192,2048]{1,0:T(8,128)(2,1)} %param.5, bf16[]{:T(256)} %constant.8.clone.1), kind=kCustom, calls=%fused_computation.5 | custom fusion | bytes 983552 | tf_op jit(solution)/shard_map/scatter | solution.py:18
  13.6 1.2 reshape.39
  14.8 4.3 %all-to-all-start.1 = ((bf16[4,60,2048]{2,1,0:T(8,128)(2,1)}), bf16[4,60,2048]{2,1,0:T(8,128)(2,1)S(1)}, u32[]{:S(2)}, u32[]{:S(2)}) async-start(bf16[4,60,2048]{2,1,0:T(8,128)(2,1)} %reshape.39), calls=%async_computation.1 | async-start | bytes 2097152 | tf_op jit(solution)/shard_map/all_to_all | solution.py:41
  19.0 2.6 %scatter_custom_fusion = bf16[240,2048]{1,0:T(8,128)(2,1)S(1)} fusion(s32[192]{0:T(256)S(1)} %bitcast.33, bf16[192,2048]{1,0:T(8,128)(2,1)} %param.6, bf16[]{:T(256)} %constant.8.clone.1), kind=kCustom, calls=%fused_computation.7 | custom fusion | bytes 983552 | tf_op jit(solution)/shard_map/scatter | solution.py:18
  21.7 0.0 copy-start
  21.7 1.2 reshape.37
  22.9 10.6 %all-to-all-done.1 = bf16[4,60,2048]{2,1,0:T(8,128)(2,1)S(1)} async-done(((bf16[4,60,2048]{2,1,0:T(8,128)(2,1)}), bf16[4,60,2048]{2,1,0:T(8,128)(2,1)S(1)}, u32[]{:S(2)}, u32[]{:S(2)}) %all-to-all-start.1) | async-done | bytes 983072 | tf_op jit(solution)/shard_map/all_to_all | solution.py:41
  33.5 3.5 %all-to-all-start = ((bf16[4,60,2048]{2,1,0:T(8,128)(2,1)}), bf16[4,60,2048]{2,1,0:T(8,128)(2,1)S(1)}, u32[]{:S(2)}, u32[]{:S(2)}) async-start(bf16[4,60,2048]{2,1,0:T(8,128)(2,1)} %reshape.37), calls=%async_computation | async-start | bytes 2097152 | tf_op jit(solution)/shard_map/all_to_all | solution.py:42
  37.0 0.0 reduce-scatter.2.cloned.1.call-start
  37.1 14.8 %all-gather = bf16[1,64,512]{2,1,0:T(8,128)(2,1)S(1)} all-gather(bf16[1,16,512]{2,1,0:T(8,128)(2,1)S(1)} %copy-done), channel_id=2, replica_groups=mesh['dp'=2,'node'=4,'local'=4] {'node'}, dimensions={1}, use_global_device_ids=true | all-gather | bytes 81920 | tf_op jit(solution)/shard_map/all_gather | solution.py:54
  51.8 0.2 reshape.40
  52.0 0.0 all-to-all-done
  52.0 1.2 reshape.38
  53.2 5.2 %all-gather.5.cloned.1.call-done = bf16[64,32,512]{2,1,0:T(8,128)(2,1)} async-done(((bf16[16,32,512]{2,1,0:T(8,128)(2,1)}), bf16[64,32,512]{2,1,0:T(8,128)(2,1)}) %all-gather.5.cloned.1.call-update) | async-done | bytes 2097168 | tf_op jit(solution)/shard_map/all_gather | solution.py:53
  58.4 2.2 %multiply_convert_fusion.1 = bf16[64,32,512]{2,1,0:T(8,128)(2,1)S(1)} fusion(bf16[64,32,512]{2,1,0:T(8,128)(2,1)} %all-gather.5.cloned.1.call-done, f32[64,512]{1,0:T(8,128)S(1)} %bitcast_convert_fusion), kind=kLoop, calls=%fused_computation.3 | loop fusion | flops 3145728 | bytes 4325376 | tf_op jit(solution)/shard_map/convert_element_type | solution.py:23
  60.6 4.0 %multiply_convert_fusion = bf16[2048,512]{1,0:T(8,128)(2,1)} fusion(bf16[240,2048]{1,0:T(8,128)(2,1)} %reshape.38, bf16[240,2048]{1,0:T(8,128)(2,1)S(1)} %reshape.40, bf16[2048,512]{1,0:T(8,128)(2,1)S(1)} %bitcast.24), kind=kOutput, calls=%fused_computation.2 | convolution fusion | flops 1009344512 | bytes 6160384 | tf_op jit(solution)/shard_map/dot_general | solution.py:27
  64.6 0.0 reduce-scatter.2.cloned.1.call-update
  64.6 0.0 all-gather.7.cloned.1.call-start
  64.7 42.5 %reduce-scatter.2.cloned.1.call-done = bf16[512,512]{1,0:T(8,128)(2,1)} async-done(((bf16[2048,512]{1,0:T(8,128)(2,1)}), bf16[512,512]{1,0:T(8,128)(2,1)}) %reduce-scatter.2.cloned.1.call-update) | async-done | bytes 524304 | tf_op jit(solution)/shard_map/reduce_scatter | solution.py:63
  107.2 0.0 all-gather.7.cloned.1.call-update
  107.2 22.0 %all-gather.7.cloned.1.call-done = bf16[1024,512]{1,0:T(8,128)(2,1)} async-done(((bf16[512,512]{1,0:T(8,128)(2,1)}), bf16[1024,512]{1,0:T(8,128)(2,1)}) %all-gather.7.cloned.1.call-update) | async-done | bytes 1048592 | tf_op jit(solution)/shard_map/all_gather | solution.py:66
  129.2 2.3 %reduce_sum.25 = bf16[512,512]{1,0:T(8,128)(2,1)} reduce(bf16[2,512,512]{2,1,0:T(8,128)(2,1)} %bitcast.25, bf16[]{:T(256)} %constant.8.clone.1), dimensions={0}, to_apply=%region_6.7 | reduce | flops 262144 | bytes 1572866 | tf_op jit(solution)/shard_map/reduce_sum | solution.py:66
  (7 shorter events, 0.1 us)
Async XLA Ops:
  6.5 51.8 %all-gather.5.cloned.1.call-start = ((), (), s32[]{:S(2)}) async-start(), calls=%async_computation.3 | async-start | bytes 2621440 | tf_op jit(solution)/shard_map/all_gather | solution.py:53
  14.8 18.7 %all-to-all-start.1 = ((bf16[4,60,2048]{2,1,0:T(8,128)(2,1)}), bf16[4,60,2048]{2,1,0:T(8,128)(2,1)S(1)}, u32[]{:S(2)}, u32[]{:S(2)}) async-start(bf16[4,60,2048]{2,1,0:T(8,128)(2,1)} %reshape.39), calls=%async_computation.1 | async-start | bytes 2097152 | tf_op jit(solution)/shard_map/all_to_all | solution.py:41
  21.7 15.4 %copy-start = (bf16[1,16,512]{2,1,0:T(8,128)(2,1)S(1)}, bf16[1,16,512]{2,1,0:T(8,128)(2,1)}, u32[]{:S(2)}) copy-start(bf16[1,16,512]{2,1,0:T(8,128)(2,1)} %param.9) | copy-start | bytes 49156
  33.5 18.6 %all-to-all-start = ((bf16[4,60,2048]{2,1,0:T(8,128)(2,1)}), bf16[4,60,2048]{2,1,0:T(8,128)(2,1)S(1)}, u32[]{:S(2)}, u32[]{:S(2)}) async-start(bf16[4,60,2048]{2,1,0:T(8,128)(2,1)} %reshape.37), calls=%async_computation | async-start | bytes 2097152 | tf_op jit(solution)/shard_map/all_to_all | solution.py:42
  37.0 70.2 %reduce-scatter.2.cloned.1.call-start = ((), (), s32[]{:S(2)}) async-start(), calls=%async_computation.4 | async-start | bytes 2621440 | tf_op jit(solution)/shard_map/reduce_scatter | solution.py:63
  64.6 64.6 %all-gather.7.cloned.1.call-start = ((), (), s32[]{:S(2)}) async-start(), calls=%async_computation.5 | async-start | bytes 1572864 | tf_op jit(solution)/shard_map/all_gather | solution.py:66
Sparse Core Ops, SparseCore 0:
  8.9 49.4 all-gather.4
  64.7 42.4 reduce-scatter.1
  108.7 20.4 all-gather.6
